TPU v7x, 32 devices: a whole 2x2x4 slice. The times are simulated.
32 devices in a mesh: tp: 8 (over y, x, core), dp: 4 (over z).
Axes of the slice: x: 2, y: 2, z: 4, core: 2. Of those that a mesh axis runs over, the one named last changes fastest.
Arguments:
- activations: bfloat16 [64, 512, 4096], P('dp', None, 'tp'), may hold values from -6 to 6
- query_output_cotangent: bfloat16 [64, 512, 4096], P('dp', None, 'tp'), may hold values from -6 to 6
- value_output_cotangent: bfloat16 [64, 512, 4096], P('dp', None, 'tp'), may hold values from -6 to 6
- lengths: int32 [64], P('dp'), may hold values from 1 to 512
- reducing_matrices_pair: bfloat16 [2, 4096, 128], P(None, 'tp'), may hold values from -0.09375 to 0.09375
- expanding_matrices_pair: bfloat16 [2, 128, 4096], P(None, None, 'tp'), may hold values from -0.5 to 0.5
- width_side_projections: bfloat16 [2, 4096, 128], P(None, 'tp'), may hold values from -0.09375 to 0.09375
- narrow_random_sketch: bfloat16 [128, 16], replicated, may hold values from -0.5 to 0.5
- projected_first_moment: float32 [8192], replicated, may hold values from -6 to 6
- projected_second_moment: float32 [8192], replicated, may hold values from 0.1 to 10
- targets: bfloat16 [1024, 8192], P('dp', 'tp'), may hold values from -6 to 6
Outputs:
- scores: float32 [64, 1024], P('dp', 'tp')
All inputs are finite; a program needn't handle non-finite values.
Results may differ from a plain program's by a relative error of at most 0.023.
Values may be sent and summed in bfloat16 or wider, within the bound.
A program may use at most 128 MiB of HBM per device.

v0:
```python
import math
import jax
import jax.numpy as jnp
from jax import lax
from jax.sharding import PartitionSpec as P


def adam_update(features, first_moment, second_moment):
    mixed = 0.9 * first_moment + 0.1 * features
    spread = 0.999 * second_moment + 0.001 * features * features
    return mixed / (jnp.sqrt(spread) + 1e-08)


def combine_factors(reducing_matrices_pair, expanding_matrices_pair, narrow_random_sketch):
    attention_key_reducer = jnp.dot(
        reducing_matrices_pair[0], narrow_random_sketch, preferred_element_type=jnp.float32
    ).astype(jnp.bfloat16)
    value_down_factor = jnp.dot(
        reducing_matrices_pair[1], narrow_random_sketch, preferred_element_type=jnp.float32
    ).astype(jnp.bfloat16)
    query_up_factor = jnp.dot(
        expanding_matrices_pair[0].T, narrow_random_sketch, preferred_element_type=jnp.float32
    ).astype(jnp.bfloat16)
    value_up_factor = jnp.dot(
        expanding_matrices_pair[1].T, narrow_random_sketch, preferred_element_type=jnp.float32
    ).astype(jnp.bfloat16)
    return (attention_key_reducer, value_down_factor, query_up_factor, value_up_factor)


def body(
    activations,
    query_output_cotangent,
    value_output_cotangent,
    lengths,
    reducing_matrices_pair,
    expanding_matrices_pair,
    width_side_projections,
    narrow_random_sketch,
    projected_first_moment,
    projected_second_moment,
    targets,
):
    attention_key_reducer, value_down_factor, query_up_factor, value_up_factor = combine_factors(
        reducing_matrices_pair, expanding_matrices_pair, narrow_random_sketch
    )
    rank_cols = narrow_random_sketch.shape[1]
    w_left = jnp.concatenate(
        [attention_key_reducer, value_down_factor, width_side_projections[0]], axis=1
    )
    w_query = jnp.concatenate([query_up_factor, width_side_projections[1]], axis=1)
    w_value = jnp.concatenate([value_up_factor, width_side_projections[1]], axis=1)
    groups = lax.axis_size("tp")
    parts = lax.axis_size("dp")
    member = lax.axis_index("tp")
    local_ex, seq_len = activations.shape[:2]
    feature_count = projected_first_moment.shape[0]
    positions = jnp.arange(seq_len, dtype=jnp.int32)
    token_mask = (positions[None, :] < lengths[:, None])[..., None]

    def project(rows, weights):
        out = jnp.einsum("esd,dc->esc", rows, weights, preferred_element_type=jnp.float32)
        return out.astype(jnp.bfloat16)

    left = project(activations, w_left)
    right_q = project(query_output_cotangent, w_query)
    right_v = project(value_output_cotangent, w_value)
    narrow = jnp.concatenate(
        [left[..., : 2 * rank_cols], right_q[..., :rank_cols], right_v[..., :rank_cols]], axis=-1
    )
    narrow = jnp.where(token_mask, narrow, jnp.zeros((), jnp.bfloat16))
    narrow = lax.psum(narrow, "tp")

    def outer_sum(first, wide):
        return jnp.einsum(
            "esr,esk->erk",
            narrow[..., first * rank_cols : (first + 1) * rank_cols],
            wide,
            preferred_element_type=jnp.float32,
        )

    own_features = jnp.concatenate(
        [
            outer_sum(2, left[..., 2 * rank_cols :]),
            outer_sum(3, left[..., 2 * rank_cols :]),
            outer_sum(0, right_q[..., rank_cols:]),
            outer_sum(1, right_v[..., rank_cols:]),
        ],
        axis=1,
    ).reshape(local_ex, -1)
    features = lax.psum_scatter(
        own_features.astype(jnp.bfloat16), "tp", scatter_dimension=1, tiled=True
    ).astype(jnp.float32)
    span = feature_count // groups
    first_moment = lax.dynamic_slice_in_dim(projected_first_moment, member * span, span)
    second_moment = lax.dynamic_slice_in_dim(projected_second_moment, member * span, span)
    update = adam_update(features, first_moment, second_moment).astype(jnp.bfloat16)
    update = lax.all_gather(update, "dp", axis=0, tiled=True)
    wide_update = update.astype(jnp.float32)
    target_float = targets.astype(jnp.float32)
    update_sq = jnp.sum(wide_update * wide_update, axis=1)
    target_sq = jnp.sum(target_float * target_float, axis=1)
    dots = lax.dot_general(
        update, targets, (((1,), (1,)), ((), ())), preferred_element_type=jnp.float32
    )
    rows = jnp.concatenate(
        [dots, jnp.broadcast_to(update_sq[:, None], (dots.shape[0], 128))], axis=1
    ).reshape(parts, local_ex, -1)
    extra = jnp.pad(target_sq, (0, 128))
    rows = jnp.concatenate([rows, jnp.broadcast_to(extra, (parts, 8, extra.shape[0]))], axis=1)
    rows = lax.psum(rows, "tp")
    rows = lax.all_to_all(rows, "dp", split_axis=0, concat_axis=0, tiled=True)
    owned = targets.shape[0]
    totals = jnp.moveaxis(rows[:, :, :owned], 0, 1).reshape(local_ex + 8, parts * owned)
    columns = parts * owned // groups
    totals = lax.dynamic_slice_in_dim(totals, member * columns, columns, 1)
    row_scale = lax.rsqrt(rows[0, :local_ex, owned : owned + 1] + 1e-06)
    column_scale = lax.rsqrt(totals[local_ex : local_ex + 1] + 1e-06)
    return totals[:local_ex] * row_scale * column_scale * math.sqrt(feature_count)


def solution(mesh):
    placed = (
        P("dp", None, "tp"),
        P("dp", None, "tp"),
        P("dp", None, "tp"),
        P("dp"),
        P(None, "tp", None),
        P(None, None, "tp"),
        P(None, "tp", None),
        P(),
        P(),
        P(),
        P("dp", "tp"),
    )
    return jax.shard_map(body, mesh=mesh, in_specs=placed, out_specs=P("dp", "tp"), check_vma=False)
```

profile of v0, /device:TPU:0, one launch (start us, length us, event | category | flops | bytes accessed | tf_op | source)
XLA Modules:
  0.0 220.2 jit_solution(16352123582546980845)
XLA Ops:
  6.5 0.7 copy-done
  7.2 1.0 convolution_convert_fusion.2
  8.3 1.1 convolution_convert_fusion.3
  9.3 1.0 convolution_convert_fusion.1
  10.4 1.0 convolution_convert_fusion
  11.4 1.0 fusion.55
  12.4 0.1 copy.37
  12.5 6.3 %convert_bitcast_fusion = bf16[16,512,160]{1,2,0:T(8,128)(2,1)S(1)} fusion(bf16[16,512,512]{2,1,0:T(8,128)(2,1)} %param.11, bf16[512,128]{0,1:T(8,128)(2,1)S(1)} %bitcast.53, bf16[512,16]{0,1:T(8,128)(2,1)S(1)} %convolution_convert_fusion.2, bf16[512,16]{0,1:T(8,128)(2,1)S(1)} %convolution_convert_fusion.3), kind=kOutput, calls=%fused_computation | convolution fusion | flops 1343979520 | bytes 11173888 | tf_op jit(solution)/shard_map/esd,dc->esc/dot_general | solution.py:61
  18.8 0.1 copy.38
  18.9 7.1 %convert_bitcast_fusion.2 = bf16[16,512,144]{1,2,0:T(8,128)(2,1)S(1)} fusion(bf16[16,512,512]{2,1,0:T(8,128)(2,1)} %param.12, bf16[512,16]{0,1:T(8,128)(2,1)S(1)} %convolution_convert_fusion.1, bf16[512,128]{0,1:T(8,128)(2,1)S(1)} %bitcast.49), kind=kOutput, calls=%fused_computation.2 | convolution fusion | flops 1209434112 | bytes 10895360 | tf_op jit(solution)/shard_map/esd,dc->esc/dot_general | solution.py:61
  26.1 7.1 %convert_bitcast_fusion.1 = bf16[16,512,144]{1,2,0:T(8,128)(2,1)S(1)} fusion(bf16[16,512,512]{2,1,0:T(8,128)(2,1)} %param.13, bf16[512,16]{0,1:T(8,128)(2,1)S(1)} %convolution_convert_fusion, bf16[512,128]{0,1:T(8,128)(2,1)S(1)} %bitcast.50), kind=kOutput, calls=%fused_computation.1 | convolution fusion | flops 1209434112 | bytes 10895360 | tf_op jit(solution)/shard_map/esd,dc->esc/dot_general | solution.py:61
  33.2 1.4 copy-done.5
  34.7 1.3 maximum_select_fusion
  36.1 59.4 %all-reduce.4.cloned.1.call-done = bf16[16,512,64]{1,2,0:T(8,128)(2,1)} async-done(((bf16[16,512,64]{1,2,0:T(8,128)(2,1)}), bf16[16,512,64]{1,2,0:T(8,128)(2,1)}) %all-reduce.4.cloned.1.call-update) | async-done | bytes 1048592 | tf_op jit(solution)/shard_map/psum | solution.py:71
  95.5 1.7 fusion.8
  97.2 1.8 fusion.11
  99.0 0.6 fusion.14
  99.7 0.7 fusion.17
  100.4 0.9 copy.42
  101.3 0.2 multiply_reduce_fusion
  101.5 0.7 dynamic-slice_multiply_fusion.1
  102.2 31.9 %reduce-scatter.2.cloned.1.call-done = bf16[16,1024]{1,0:T(8,128)(2,1)} async-done(((bf16[16,8192]{1,0:T(8,128)(2,1)}), bf16[16,1024]{1,0:T(8,128)(2,1)}) %reduce-scatter.2.cloned.1.call-update) | async-done | bytes 32784 | tf_op jit(solution)/shard_map/reduce_scatter | solution.py:90
  134.1 0.8 fusion.42
  134.9 13.5 %all_gather.3 = bf16[64,1024]{1,0:T(8,128)(2,1)S(1)} all-gather(bf16[16,1024]{1,0:T(8,128)(2,1)S(1)} %fusion.42), channel_id=1, replica_groups=mesh['tp'=8,'dp'=4] {'dp'}, dimensions={0}, use_global_device_ids=true | all-gather | bytes 163840 | tf_op jit(solution)/shard_map/all_gather | solution.py:97
  148.4 0.3 fusion.56
  148.7 0.1 multiply_reduce_fusion.1
  148.9 0.7 pad_maximum_fusion.1
  149.6 52.0 %all-reduce.6.cloned.1.call-done = f32[4,24,384]{2,1,0:T(8,128)} async-done(((f32[4,24,384]{2,1,0:T(8,128)}), f32[4,24,384]{2,1,0:T(8,128)}) %all-reduce.6.cloned.1.call-update) | async-done | bytes 147472 | tf_op jit(solution)/shard_map/psum | solution.py:110
  201.6 4.6 %all-to-all-start = ((f32[4,24,384]{2,1,0:T(8,128)}), f32[4,24,384]{2,1,0:T(8,128)S(1)}, u32[]{:S(2)}, u32[]{:S(2)}) async-start(f32[4,24,384]{2,1,0:T(8,128)} %all-reduce.6.cloned.1.call-done), calls=%async_computation.1 | async-start | bytes 294912 | tf_op jit(solution)/shard_map/all_to_all | solution.py:111
  206.2 6.6 %all-to-all-done = f32[4,24,384]{2,1,0:T(8,128)S(1)} async-done(((f32[4,24,384]{2,1,0:T(8,128)}), f32[4,24,384]{2,1,0:T(8,128)S(1)}, u32[]{:S(2)}, u32[]{:S(2)}) %all-to-all-start) | async-done | bytes 147488 | tf_op jit(solution)/shard_map/all_to_all | solution.py:111
  212.9 0.1 fusion.47
  213.0 0.7 fusion.49
  (37 shorter events, 0.5 us)
Async XLA Ops:
  6.5 0.7 copy-start
  6.5 88.9 %all-reduce.4.cloned.1.call-start = ((), (), s32[]{:S(2)}) async-start(), calls=%async_computation.2 | async-start | bytes 2097152 | tf_op jit(solution)/shard_map/psum | solution.py:71
  18.8 7.2 %copy-start.1 = (bf16[16,512,160]{1,2,0:T(8,128)(2,1)}, bf16[16,512,160]{1,2,0:T(8,128)(2,1)S(1)}, u32[]{:S(2)}) copy-start(bf16[16,512,160]{1,2,0:T(8,128)(2,1)S(1)} %convert_bitcast_fusion) | copy-start | bytes 7864324
  26.0 7.2 %copy-start.3 = (bf16[16,512,144]{1,2,0:T(8,128)(2,1)}, bf16[16,512,144]{1,2,0:T(8,128)(2,1)S(1)}, u32[]{:S(2)}) copy-start(bf16[16,512,144]{1,2,0:T(8,128)(2,1)S(1)} %convert_bitcast_fusion.2) | copy-start | bytes 7077892
  26.1 8.6 %copy-start.8 = (s32[16]{0:T(128)S(1)}, s32[16]{0:T(128)}, u32[]{:S(2)}) copy-start(s32[16]{0:T(128)} %param.14) | copy-start | bytes 196
  26.1 8.6 %slice-start = ((bf16[16,512,160]{1,2,0:T(8,128)(2,1)}), bf16[16,512,32]{1,2,0:T(8,128)(2,1)S(1)}, s32[]{:S(2)}) async-start(bf16[16,512,160]{1,2,0:T(8,128)(2,1)} %copy-done.1), calls=%async_computation.5 | async-start | bytes 1048576 | tf_op jit(solution)/shard_map/slice | solution.py:68
  33.2 1.4 copy-start.5
  33.2 62.3 %copy-start.2 = (bf16[16,512,160]{1,2,0:T(8,128)(2,1)S(1)}, bf16[16,512,160]{1,2,0:T(8,128)(2,1)}, u32[]{:S(2)}) copy-start(bf16[16,512,160]{1,2,0:T(8,128)(2,1)} %copy-done.1) | copy-start | bytes 7864324
  36.0 98.1 %reduce-scatter.2.cloned.1.call-start = ((), (), s32[]{:S(2)}) async-start(), calls=%async_computation.3 | async-start | bytes 294912 | tf_op jit(solution)/shard_map/reduce_scatter | solution.py:90
  95.5 3.5 %copy-start.4 = (bf16[16,512,144]{1,2,0:T(8,128)(2,1)S(1)}, bf16[16,512,144]{1,2,0:T(8,128)(2,1)}, u32[]{:S(2)}) copy-start(bf16[16,512,144]{1,2,0:T(8,128)(2,1)} %copy-done.3) | copy-start | bytes 7077892
  95.5 3.5 %copy-start.9 = (bf16[16,512,64]{1,2,0:T(8,128)(2,1)S(1)}, bf16[16,512,64]{1,2,0:T(8,128)(2,1)}, u32[]{:S(2)}) copy-start(bf16[16,512,64]{1,2,0:T(8,128)(2,1)} %all-reduce.4.cloned.1.call-done) | copy-start | bytes 3145732
  97.2 2.4 %copy-start.6 = (bf16[16,512,144]{1,2,0:T(8,128)(2,1)S(1)}, bf16[16,512,144]{1,2,0:T(8,128)(2,1)}, u32[]{:S(2)}) copy-start(bf16[16,512,144]{1,2,0:T(8,128)(2,1)} %copy-done.5) | copy-start | bytes 7077892
  99.0 2.3 %copy-start.7 = (bf16[256,1024]{1,0:T(8,128)(2,1)S(1)}, bf16[256,1024]{1,0:T(8,128)(2,1)}, u32[]{:S(2)}) copy-start(bf16[256,1024]{1,0:T(8,128)(2,1)} %param.21) | copy-start | bytes 1572868
  101.3 100.4 %all-reduce.6.cloned.1.call-start = ((), (), s32[]{:S(2)}) async-start(), calls=%async_computation.4 | async-start | bytes 294912 | tf_op jit(solution)/shard_map/psum | solution.py:110
  201.6 11.2 %all-to-all-start = ((f32[4,24,384]{2,1,0:T(8,128)}), f32[4,24,384]{2,1,0:T(8,128)S(1)}, u32[]{:S(2)}, u32[]{:S(2)}) async-start(f32[4,24,384]{2,1,0:T(8,128)} %all-reduce.6.cloned.1.call-done), calls=%async_computation.1 | async-start | bytes 294912 | tf_op jit(solution)/shard_map/all_to_all | solution.py:111
Sparse Core Ops, SparseCore 0:
  36.1 59.2 all-reduce.3
  101.4 32.6 reduce-scatter.1
  149.8 51.8 all-reduce.5
where the time goes:
time: 221 us; the launch traced here: 220 us
  waiting for transfers between devices  150 us (68%)
  matrix products  29.7 us (13%)
  blocking collectives  13.5 us (6%)
  between operations  13.3 us (6%)
  other arithmetic  4.71 us (2%)
  starting transfers between devices  4.69 us (2%)
  local copies, waits for them, and re-layouts  4.36 us (2%)
    psum x1, waiting for transfers between devices, body(): narrow = lax.psum(narrow, 'tp')  59.4 us
    psum x1, waiting for transfers between devices, body(): rows = lax.psum(rows, 'tp')  52 us
    reduce_scatter x1, waiting for transfers between devices, body(): lax.psum_scatter(own_features.astype(jnp.bfloat16), 'tp', scatter_dimensi...  31.9 us
    dot_general x3, matrix products, project(): jnp.einsum('esd,dc->esc', rows, weights, preferred_element_type=jnp.float32)  20.4 us
    all_gather x1, blocking collectives, body(): update = lax.all_gather(update, 'dp', axis=0, tiled=True)  13.5 us
    all_to_all x1, waiting for transfers between devices, body(): rows = lax.all_to_all(rows, 'dp', split_axis=0, concat_axis=0, tiled=True)  6.65 us
    dot_general x4, matrix products, outer_sum(): jnp.einsum('esr,esk->erk', narrow[..., first * rank_cols:(first + 1) * ra...  4.82 us
    all_to_all x1, starting transfers between devices, body(): rows = lax.all_to_all(rows, 'dp', split_axis=0, concat_axis=0, tiled=True)  4.6 us
  transfers between devices with their start and end apart: 4, of which 4 were waited for; matrix products, arithmetic and copies ran while one was open for 0% of the time, Pallas kernels for 0%

commit v1 on v0

--- a/solution.py
+++ b/solution.py
@@ -94,7 +94,21 @@
     first_moment = lax.dynamic_slice_in_dim(projected_first_moment, member * span, span)
     second_moment = lax.dynamic_slice_in_dim(projected_second_moment, member * span, span)
     update = adam_update(features, first_moment, second_moment).astype(jnp.bfloat16)
-    update = lax.all_gather(update, "dp", axis=0, tiled=True)
+    ways, here, step = (lax.axis_size("dp"), lax.axis_index("dp"), update.shape[0])
+    lengths_2 = [n * ways if d == 0 else n for d, n in enumerate(update.shape)]
+    full = lax.dynamic_update_slice_in_dim(
+        jnp.zeros(lengths_2, update.dtype), update, here * step, axis=0
+    )
+    going_up = going_down = update
+    for far in range(1, ways // 2 + 1):
+        going_up = lax.ppermute(going_up, "dp", [(d, (d + 1) % ways) for d in range(ways)])
+        full = lax.dynamic_update_slice_in_dim(full, going_up, (here - far) % ways * step, axis=0)
+        if 2 * far < ways:
+            going_down = lax.ppermute(going_down, "dp", [(d, (d - 1) % ways) for d in range(ways)])
+            full = lax.dynamic_update_slice_in_dim(
+                full, going_down, (here + far) % ways * step, axis=0
+            )
+    update = full
     wide_update = update.astype(jnp.float32)
     target_float = targets.astype(jnp.float32)
     update_sq = jnp.sum(wide_update * wide_update, axis=1)

time: 221 us -> 216 us (0.977)
  blocking collectives: 13.5 us -> 0 us
  waiting for transfers between devices: 150 us -> 155 us
  starting transfers between devices: 4.69 us -> 8.62 us
    all_gather x1 -> x0, blocking collectives: 13.5 us -> none  [body(): update = lax.all_gather(update, 'dp', axis=0, tiled=True)]
    ppermute x0 -> x3, waiting for transfers between devices: none -> 7.6 us  [the longest x2 7.59 us: body(): lax.ppermute(going_up, 'dp', [(d, (d + 1) % ways) for d in range(ways)])]
    ppermute x0 -> x3, starting transfers between devices: none -> 3.93 us  [the longest x1 2.4 us: body(): lax.ppermute(going_down, 'dp', [(d, (d - 1) % ways) for d in range(ways)])]
    psum x1, waiting for transfers between devices: 52 us -> 49.3 us  [body(): rows = lax.psum(rows, 'tp')]
  transfers between devices with their start and end apart: 4 -> 7, of which waited for: 4 -> 6; matrix products, arithmetic and copies ran while one was open for 0% -> 0% of each run, Pallas kernels for 0% -> 0%
where the time goes in v1:
time: 216 us
  waiting for transfers between devices  155 us (72%)
  matrix products  29.7 us (14%)
  between operations  13.4 us (6%)
  starting transfers between devices  8.62 us (4%)
  other arithmetic  4.73 us (2%)
  local copies, waits for them, and re-layouts  4.39 us (2%)
    psum x1, waiting for transfers between devices, body(): narrow = lax.psum(narrow, 'tp')  59.4 us
    psum x1, waiting for transfers between devices, body(): rows = lax.psum(rows, 'tp')  49.3 us
    reduce_scatter x1, waiting for transfers between devices, body(): lax.psum_scatter(own_features.astype(jnp.bfloat16), 'tp', scatter_dimensi...  32.1 us
    dot_general x3, matrix products, project(): jnp.einsum('esd,dc->esc', rows, weights, preferred_element_type=jnp.float32)  20.4 us
    ppermute x2, waiting for transfers between devices, body(): lax.ppermute(going_up, 'dp', [(d, (d + 1) % ways) for d in range(ways)])  7.59 us
    all_to_all x1, waiting for transfers between devices, body(): rows = lax.all_to_all(rows, 'dp', split_axis=0, concat_axis=0, tiled=True)  6.65 us
    dot_general x4, matrix products, outer_sum(): jnp.einsum('esr,esk->erk', narrow[..., first * rank_cols:(first + 1) * ra...  4.83 us
    all_to_all x1, starting transfers between devices, body(): rows = lax.all_to_all(rows, 'dp', split_axis=0, concat_axis=0, tiled=True)  4.6 us
  transfers between devices with their start and end apart: 7, of which 6 were waited for; matrix products, arithmetic and copies ran while one was open for 0% of the time, Pallas kernels for 0%

profile of v1, /device:TPU:0, one launch (start us, length us, event | category | flops | bytes accessed | tf_op | source)
XLA Modules:
  0.0 215.9 jit_solution(307987081440048355)
XLA Ops:
  6.5 0.7 copy-done
  7.2 1.0 convolution_convert_fusion.2
  8.3 1.1 convolution_convert_fusion.3
  9.3 1.0 convolution_convert_fusion.1
  10.4 1.0 convolution_convert_fusion
  11.4 1.0 fusion.56
  12.5 6.3 %convert_bitcast_fusion = bf16[16,512,160]{1,2,0:T(8,128)(2,1)S(1)} fusion(bf16[16,512,512]{2,1,0:T(8,128)(2,1)} %param.11, bf16[512,128]{0,1:T(8,128)(2,1)S(1)} %bitcast.53, bf16[512,16]{0,1:T(8,128)(2,1)S(1)} %convolution_convert_fusion.2, bf16[512,16]{0,1:T(8,128)(2,1)S(1)} %convolution_convert_fusion.3), kind=kOutput, calls=%fused_computation | convolution fusion | flops 1343979520 | bytes 11173888 | tf_op jit(solution)/shard_map/esd,dc->esc/dot_general | solution.py:61
  18.9 7.1 %convert_bitcast_fusion.2 = bf16[16,512,144]{1,2,0:T(8,128)(2,1)S(1)} fusion(bf16[16,512,512]{2,1,0:T(8,128)(2,1)} %param.12, bf16[512,16]{0,1:T(8,128)(2,1)S(1)} %convolution_convert_fusion.1, bf16[512,128]{0,1:T(8,128)(2,1)S(1)} %bitcast.49), kind=kOutput, calls=%fused_computation.2 | convolution fusion | flops 1209434112 | bytes 10895360 | tf_op jit(solution)/shard_map/esd,dc->esc/dot_general | solution.py:61
  26.1 7.1 %convert_bitcast_fusion.1 = bf16[16,512,144]{1,2,0:T(8,128)(2,1)S(1)} fusion(bf16[16,512,512]{2,1,0:T(8,128)(2,1)} %param.13, bf16[512,16]{0,1:T(8,128)(2,1)S(1)} %convolution_convert_fusion, bf16[512,128]{0,1:T(8,128)(2,1)S(1)} %bitcast.50), kind=kOutput, calls=%fused_computation.1 | convolution fusion | flops 1209434112 | bytes 10895360 | tf_op jit(solution)/shard_map/esd,dc->esc/dot_general | solution.py:61
  33.2 1.4 copy-done.5
  34.7 1.3 maximum_select_fusion
  36.1 59.4 %all-reduce.4.cloned.1.call-done = bf16[16,512,64]{1,2,0:T(8,128)(2,1)} async-done(((bf16[16,512,64]{1,2,0:T(8,128)(2,1)}), bf16[16,512,64]{1,2,0:T(8,128)(2,1)}) %all-reduce.4.cloned.1.call-update) | async-done | bytes 1048592 | tf_op jit(solution)/shard_map/psum | solution.py:71
  95.5 1.7 fusion.8
  97.2 1.8 fusion.11
  99.0 0.7 fusion.14
  99.7 0.7 fusion.17
  100.4 0.9 copy.42
  101.3 0.7 dynamic-slice_multiply_fusion.1
  102.1 32.1 %reduce-scatter.2.cloned.1.call-done = bf16[16,1024]{1,0:T(8,128)(2,1)} async-done(((bf16[16,8192]{1,0:T(8,128)(2,1)}), bf16[16,1024]{1,0:T(8,128)(2,1)}) %reduce-scatter.2.cloned.1.call-update) | async-done | bytes 32784 | tf_op jit(solution)/shard_map/reduce_scatter | solution.py:90
  134.2 0.8 constant_dynamic-update-slice_fusion.3
  135.0 1.5 collective-permute-start
  136.5 0.2 multiply_reduce_fusion
  136.8 2.4 %collective-permute-start.1 = (bf16[16,1024]{1,0:T(8,128)(2,1)S(1)}, bf16[16,1024]{1,0:T(8,128)(2,1)S(1)}, u32[]{:S(2)}, u32[]{:S(2)}) collective-permute-start(bf16[16,1024]{1,0:T(8,128)(2,1)S(1)} %get-tuple-element.6), channel_id=1, source_target_pairs={{0,3},{1,0},{2,1},{3,2},{4,7},{5,4},{6,5},{7,6},{8,11},{9,8},{10,9... | collective-permute-start | bytes 98312 | tf_op jit(solution)/shard_map/ppermute | solution.py:107
  139.1 1.9 collective-permute-done
  141.1 5.7 %collective-permute-done.2 = bf16[16,1024]{1,0:T(8,128)(2,1)S(1)} collective-permute-done((bf16[16,1024]{1,0:T(8,128)(2,1)S(1)}, bf16[16,1024]{1,0:T(8,128)(2,1)S(1)}, u32[]{:S(2)}, u32[]{:S(2)}) %collective-permute-start.2) | collective-permute-done | bytes 32800 | tf_op jit(solution)/shard_map/ppermute | solution.py:104
  146.8 0.3 fusion.57
  147.1 0.1 multiply_reduce_fusion.1
  147.3 0.7 pad_maximum_fusion.1
  148.0 49.3 %all-reduce.6.cloned.1.call-done = f32[4,24,384]{2,1,0:T(8,128)} async-done(((f32[4,24,384]{2,1,0:T(8,128)}), f32[4,24,384]{2,1,0:T(8,128)}) %all-reduce.6.cloned.1.call-update) | async-done | bytes 147472 | tf_op jit(solution)/shard_map/psum | solution.py:124
  197.3 4.6 %all-to-all-start = ((f32[4,24,384]{2,1,0:T(8,128)}), f32[4,24,384]{2,1,0:T(8,128)S(1)}, u32[]{:S(2)}, u32[]{:S(2)}) async-start(f32[4,24,384]{2,1,0:T(8,128)} %all-reduce.6.cloned.1.call-done), calls=%async_computation.1 | async-start | bytes 294912 | tf_op jit(solution)/shard_map/all_to_all | solution.py:125
  201.9 6.6 %all-to-all-done = f32[4,24,384]{2,1,0:T(8,128)S(1)} async-done(((f32[4,24,384]{2,1,0:T(8,128)}), f32[4,24,384]{2,1,0:T(8,128)S(1)}, u32[]{:S(2)}, u32[]{:S(2)}) %all-to-all-start) | async-done | bytes 147488 | tf_op jit(solution)/shard_map/all_to_all | solution.py:125
  208.7 0.7 fusion.49
  (46 shorter events, 0.8 us)
Async XLA Ops:
  6.5 0.7 copy-start
  6.5 88.9 %all-reduce.4.cloned.1.call-start = ((), (), s32[]{:S(2)}) async-start(), calls=%async_computation.2 | async-start | bytes 2097152 | tf_op jit(solution)/shard_map/psum | solution.py:71
  18.8 7.2 %copy-start.1 = (bf16[16,512,160]{1,2,0:T(8,128)(2,1)}, bf16[16,512,160]{1,2,0:T(8,128)(2,1)S(1)}, u32[]{:S(2)}) copy-start(bf16[16,512,160]{1,2,0:T(8,128)(2,1)S(1)} %convert_bitcast_fusion) | copy-start | bytes 7864324
  26.0 7.2 %copy-start.3 = (bf16[16,512,144]{1,2,0:T(8,128)(2,1)}, bf16[16,512,144]{1,2,0:T(8,128)(2,1)S(1)}, u32[]{:S(2)}) copy-start(bf16[16,512,144]{1,2,0:T(8,128)(2,1)S(1)} %convert_bitcast_fusion.2) | copy-start | bytes 7077892
  26.1 8.6 %copy-start.8 = (s32[16]{0:T(128)S(1)}, s32[16]{0:T(128)}, u32[]{:S(2)}) copy-start(s32[16]{0:T(128)} %param.14) | copy-start | bytes 196
  26.1 8.6 %slice-start = ((bf16[16,512,160]{1,2,0:T(8,128)(2,1)}), bf16[16,512,32]{1,2,0:T(8,128)(2,1)S(1)}, s32[]{:S(2)}) async-start(bf16[16,512,160]{1,2,0:T(8,128)(2,1)} %copy-done.1), calls=%async_computation.5 | async-start | bytes 1048576 | tf_op jit(solution)/shard_map/slice | solution.py:68
  33.2 1.4 copy-start.5
  33.2 62.3 %copy-start.2 = (bf16[16,512,160]{1,2,0:T(8,128)(2,1)S(1)}, bf16[16,512,160]{1,2,0:T(8,128)(2,1)}, u32[]{:S(2)}) copy-start(bf16[16,512,160]{1,2,0:T(8,128)(2,1)} %copy-done.1) | copy-start | bytes 7864324
  36.0 98.1 %reduce-scatter.2.cloned.1.call-start = ((), (), s32[]{:S(2)}) async-start(), calls=%async_computation.3 | async-start | bytes 294912 | tf_op jit(solution)/shard_map/reduce_scatter | solution.py:90
  95.5 3.5 %copy-start.4 = (bf16[16,512,144]{1,2,0:T(8,128)(2,1)S(1)}, bf16[16,512,144]{1,2,0:T(8,128)(2,1)}, u32[]{:S(2)}) copy-start(bf16[16,512,144]{1,2,0:T(8,128)(2,1)} %copy-done.3) | copy-start | bytes 7077892
  95.5 3.5 %copy-start.9 = (bf16[16,512,64]{1,2,0:T(8,128)(2,1)S(1)}, bf16[16,512,64]{1,2,0:T(8,128)(2,1)}, u32[]{:S(2)}) copy-start(bf16[16,512,64]{1,2,0:T(8,128)(2,1)} %all-reduce.4.cloned.1.call-done) | copy-start | bytes 3145732
  97.2 2.4 %copy-start.6 = (bf16[16,512,144]{1,2,0:T(8,128)(2,1)S(1)}, bf16[16,512,144]{1,2,0:T(8,128)(2,1)}, u32[]{:S(2)}) copy-start(bf16[16,512,144]{1,2,0:T(8,128)(2,1)} %copy-done.5) | copy-start | bytes 7077892
  99.7 36.8 %copy-start.7 = (bf16[256,1024]{1,0:T(8,128)(2,1)S(1)}, bf16[256,1024]{1,0:T(8,128)(2,1)}, u32[]{:S(2)}) copy-start(bf16[256,1024]{1,0:T(8,128)(2,1)} %param.21) | copy-start | bytes 1572868
  101.3 96.0 %all-reduce.6.cloned.1.call-start = ((), (), s32[]{:S(2)}) async-start(), calls=%async_computation.4 | async-start | bytes 294912 | tf_op jit(solution)/shard_map/psum | solution.py:124
  135.0 6.1 %collective-permute-start = (bf16[16,1024]{1,0:T(8,128)(2,1)S(1)}, bf16[16,1024]{1,0:T(8,128)(2,1)S(1)}, u32[]{:S(2)}, u32[]{:S(2)}) collective-permute-start(bf16[16,1024]{1,0:T(8,128)(2,1)S(1)} %get-tuple-element.6), channel_id=1, source_target_pairs={{0,1},{1,2},{2,3},{3,0},{4,5},{5,6},{6,7},{7,4},{8,9},{9,10},{10,1... | collective-permute-start | bytes 98312 | tf_op jit(solution)/shard_map/ppermute | solution.py:104
  136.8 4.3 %collective-permute-start.1 = (bf16[16,1024]{1,0:T(8,128)(2,1)S(1)}, bf16[16,1024]{1,0:T(8,128)(2,1)S(1)}, u32[]{:S(2)}, u32[]{:S(2)}) collective-permute-start(bf16[16,1024]{1,0:T(8,128)(2,1)S(1)} %get-tuple-element.6), channel_id=1, source_target_pairs={{0,3},{1,0},{2,1},{3,2},{4,7},{5,4},{6,5},{7,6},{8,11},{9,8},{10,9... | collective-permute-start | bytes 98312 | tf_op jit(solution)/shard_map/ppermute | solution.py:107
  141.1 5.7 %collective-permute-start.2 = (bf16[16,1024]{1,0:T(8,128)(2,1)S(1)}, bf16[16,1024]{1,0:T(8,128)(2,1)S(1)}, u32[]{:S(2)}, u32[]{:S(2)}) collective-permute-start(bf16[16,1024]{1,0:T(8,128)(2,1)S(1)} %collective-permute-done), channel_id=1, source_target_pairs={{0,1},{1,2},{2,3},{3,0},{4,5},{5,6},{6,7},{7,4},{8,9},{9,10},{10,1... | collective-permute-start | bytes 98312 | tf_op jit(solution)/shard_map/ppermute | solution.py:104
  197.3 11.2 %all-to-all-start = ((f32[4,24,384]{2,1,0:T(8,128)}), f32[4,24,384]{2,1,0:T(8,128)S(1)}, u32[]{:S(2)}, u32[]{:S(2)}) async-start(f32[4,24,384]{2,1,0:T(8,128)} %all-reduce.6.cloned.1.call-done), calls=%async_computation.1 | async-start | bytes 294912 | tf_op jit(solution)/shard_map/all_to_all | solution.py:125
Sparse Core Ops, SparseCore 0:
  36.2 59.2 all-reduce.3
  101.4 32.6 reduce-scatter.1
  148.1 49.1 all-reduce.5
